TPU v7x, 32 devices: a whole 2x2x4 slice. The times are simulated.
32 devices in a mesh: ctx: 8 (over z, y), mp: 4 (over x, core).
Axes of the slice: x: 2, y: 2, z: 4, core: 2. Of those that a mesh axis runs over, the one named last changes fastest.
Arguments:
- tokens: bfloat16 [3072, 6144], P('ctx', 'mp'), may hold values from -24 to 24, as said below
- qkv_weight: bfloat16 [6144, 3, 24, 128], P('ctx', None, 'mp'), may hold values from -1 to 1, as said below
Outputs:
- attended: bfloat16 [3072, 24, 128], P('ctx', 'mp')
Inputs may be any that keep to these rules, and one draw needn't show every extreme that they name: `tokens`: finite values. `qkv_weight`: entries lie within 8 / sqrt(6144) of zero.
All inputs are finite; a program needn't handle non-finite values.
Results may differ from a plain program's by a relative error of at most 0.0045.
The roundings to bfloat16 on the way count: a program that leaves them out, or rounds other values in their place, can miss the bound.
Values may be sent and summed in bfloat16 or wider, within the bound.
No kernel may reach another device: no remote copies, remote signals or barrier semaphores. Data moves between devices by JAX's collectives and lax.ppermute only.
A program may use at most 128 MiB of HBM per device.

v0:
```python
import math
import jax
import jax.numpy as jnp
from jax import lax
from jax.sharding import PartitionSpec as P

REACH = 4


def shifted(array, axis, by):
    devices = lax.axis_size(axis)
    return lax.ppermute(array, axis, [(i, (i + by) % devices) for i in range(devices)])


def collect_blocks(key_value):
    blocks = [key_value]
    current = key_value
    for step in range(1, REACH):
        current = shifted(current, "ctx", 1)
        blocks.append(current)
    return blocks


def on_device(tokens, qkv_weight):
    features = lax.all_gather(tokens, "mp", axis=1, tiled=True)
    rows_dev = features.shape[0]
    heads_local = qkv_weight.shape[2]
    head_size = qkv_weight.shape[3]
    scale = 1.0 / math.sqrt(head_size)
    piece = lax.all_gather(qkv_weight, "ctx", axis=0, tiled=True)
    flat_piece = piece.reshape(piece.shape[0], -1)
    full_total = jnp.dot(features, flat_piece, preferred_element_type=jnp.float32)
    projected = full_total.astype(jnp.bfloat16).reshape(rows_dev, 3, heads_local, head_size)
    queries = projected[:, 0]
    key_value = projected[:, 1:]
    blocks = collect_blocks(key_value)
    key_rows = jnp.concatenate([block[:, 0] for block in blocks], axis=0)
    value_rows = jnp.concatenate([block[:, 1] for block in blocks], axis=0)
    scores = (
        jnp.einsum("thd,shd->hts", queries, key_rows, preferred_element_type=jnp.float32) * scale
    )
    top = jnp.max(scores, axis=-1, keepdims=True)
    expo = jnp.exp(scores - top)
    totals = jnp.sum(expo, axis=-1, keepdims=True)
    probs = expo.astype(jnp.bfloat16)
    mixed = (
        jnp.einsum("hts,shd->htd", probs, value_rows, preferred_element_type=jnp.float32) / totals
    )
    return jnp.transpose(mixed, (1, 0, 2)).astype(jnp.bfloat16)


def solution(mesh):
    placed = (P("ctx", "mp"), P("ctx", None, "mp", None))
    return jax.shard_map(
        on_device, mesh=mesh, in_specs=placed, out_specs=P("ctx", "mp", None), check_vma=False
    )
```

profile of v0, /device:TPU:0, one launch (start us, length us, event | category | flops | bytes accessed | tf_op | source)
XLA Modules:
  0.0 727.5 jit_solution(14110665750935580521)
XLA Ops:
  6.5 0.0 all-gather.3.cloned.1.call-start
  6.5 0.7 all-gather.3.cloned.1.call-update
  7.3 0.0 all-gather.5.cloned.1.call-start
  7.3 6.1 copy.7
  13.4 0.0 all-gather.5.cloned.1.call-update
  13.4 35.7 %all-gather.3.cloned.1.call-done = bf16[384,6144]{1,0:T(8,128)(2,1)} async-done(((bf16[384,1536]{1,0:T(8,128)(2,1)}), bf16[384,6144]{1,0:T(8,128)(2,1)}) %all-gather.3.cloned.1.call-update) | async-done | bytes 4718608 | tf_op jit(solution)/shard_map/all_gather | solution.py:25
  49.1 541.0 %all-gather.5.cloned.1.call-done = bf16[6144,3,6,128]{0,3,2,1:T(8,128)(2,1)} async-done(((bf16[768,3,6,128]{0,3,2,1:T(8,128)(2,1)}), bf16[6144,3,6,128]{0,3,2,1:T(8,128)(2,1)}) %all-gather.5.cloned.1.call-update) | async-done | bytes 28311568 | tf_op jit(solution)/shard_map/all_gather | solution.py:30
  590.1 16.6 %convolution_convert_fusion = bf16[384,2304]{1,0:T(8,128)(2,1)S(1)} fusion(bf16[384,6144]{1,0:T(8,128)(2,1)} %all-gather.3.cloned.1.call-done, bf16[6144,2304]{0,1:T(8,128)(2,1)} %bitcast.35), kind=kOutput, calls=%fused_computation.7 | convolution fusion | flops 10872520704 | bytes 34799616 | tf_op jit(solution)/shard_map/dot_general | solution.py:32
  606.7 1.1 copy.8
  607.8 0.1 slice.44
  608.0 1.5 copy.15
  609.4 0.3 collective-permute-start
  609.8 30.3 %collective-permute-done = bf16[384,2,6,128]{3,0,2,1:T(8,128)(2,1)S(1)} collective-permute-done((bf16[384,2,6,128]{3,0,2,1:T(8,128)(2,1)}, bf16[384,2,6,128]{3,0,2,1:T(8,128)(2,1)S(1)}, u32[]{:S(2)}, u32[]{:S(2)}) %collective-permute-start) | collective-permute-done | bytes 1179680 | tf_op jit(solution)/shard_map/ppermute | solution.py:12
  640.0 0.0 copy-start
  640.0 0.0 collective-permute-start.1
  640.0 29.6 %collective-permute-done.1 = bf16[384,2,6,128]{3,0,2,1:T(8,128)(2,1)} collective-permute-done((bf16[384,2,6,128]{3,0,2,1:T(8,128)(2,1)S(1)}, bf16[384,2,6,128]{3,0,2,1:T(8,128)(2,1)}, u32[]{:S(2)}, u32[]{:S(2)}) %collective-permute-start.1) | collective-permute-done | bytes 1179680 | tf_op jit(solution)/shard_map/ppermute | solution.py:12
  669.7 0.0 copy-done
  669.7 0.0 collective-permute-start.2
  669.7 0.1 fusion.33
  669.8 0.3 copy.14
  670.1 0.3 copy.16
  670.4 1.3 slice_bitcast_fusion.5
  671.8 1.3 slice_bitcast_fusion.4
  673.1 25.5 %collective-permute-done.2 = bf16[384,2,6,128]{3,0,2,1:T(8,128)(2,1)} collective-permute-done((bf16[384,2,6,128]{3,0,2,1:T(8,128)(2,1)}, bf16[384,2,6,128]{3,0,2,1:T(8,128)(2,1)}, u32[]{:S(2)}, u32[]{:S(2)}) %collective-permute-start.2) | collective-permute-done | bytes 1179680 | tf_op jit(solution)/shard_map/ppermute | solution.py:12
  698.6 1.3 slice_bitcast_fusion.3
  699.9 6.2 multiply_reduce_fusion
  706.1 7.5 %fusion = f32[6,384]{1,0:T(8,128)S(1)} fusion(f32[6,384,1536]{2,1,0:T(8,128)} %get-tuple-element.14, f32[6,384]{1,0:T(8,128)S(1)} %get-tuple-element.13), kind=kLoop, calls=%fused_computation.2 | loop fusion | flops 10614528 | bytes 14174208 | tf_op jit(solution)/shard_map/reduce_sum | solution.py:44
  713.6 7.1 divide_convert_fusion
Async XLA Ops:
  6.5 42.6 %all-gather.3.cloned.1.call-start = ((), (), s32[]{:S(2)}) async-start(), calls=%async_computation | async-start | bytes 5898240 | tf_op jit(solution)/shard_map/all_gather | solution.py:25
  7.3 582.8 %all-gather.5.cloned.1.call-start = ((), (), s32[]{:S(2)}) async-start(), calls=%async_computation.1 | async-start | bytes 31850496 | tf_op jit(solution)/shard_map/all_gather | solution.py:30
  609.4 30.6 %collective-permute-start = (bf16[384,2,6,128]{3,0,2,1:T(8,128)(2,1)}, bf16[384,2,6,128]{3,0,2,1:T(8,128)(2,1)S(1)}, u32[]{:S(2)}, u32[]{:S(2)}) collective-permute-start(bf16[384,2,6,128]{3,0,2,1:T(8,128)(2,1)} %copy.15), channel_id=1, source_target_pairs={{0,4},{4,8},{8,12},{12,16},{16,20},{20,24},{24,28},{28,0},{1,5},{5... | collective-permute-start | bytes 3538952 | tf_op jit(solution)/shard_map/ppermute | solution.py:12
  640.0 29.6 %copy-start = (bf16[384,2,6,128]{3,0,2,1:T(8,128)(2,1)}, bf16[384,2,6,128]{3,0,2,1:T(8,128)(2,1)S(1)}, u32[]{:S(2)}) copy-start(bf16[384,2,6,128]{3,0,2,1:T(8,128)(2,1)S(1)} %collective-permute-done) | copy-start | bytes 3538948
  640.0 29.6 %collective-permute-start.1 = (bf16[384,2,6,128]{3,0,2,1:T(8,128)(2,1)S(1)}, bf16[384,2,6,128]{3,0,2,1:T(8,128)(2,1)}, u32[]{:S(2)}, u32[]{:S(2)}) collective-permute-start(bf16[384,2,6,128]{3,0,2,1:T(8,128)(2,1)S(1)} %collective-permute-done), channel_id=1, source_target_pairs={{0,4},{4,8},{8,12},{12,16},{16,20},{20,24},{24,28},{28,0},{1,5},{5... | collective-permute-start | bytes 3538952 | tf_op jit(solution)/shard_map/ppermute | solution.py:12
  669.7 28.9 %collective-permute-start.2 = (bf16[384,2,6,128]{3,0,2,1:T(8,128)(2,1)}, bf16[384,2,6,128]{3,0,2,1:T(8,128)(2,1)}, u32[]{:S(2)}, u32[]{:S(2)}) collective-permute-start(bf16[384,2,6,128]{3,0,2,1:T(8,128)(2,1)} %collective-permute-done.1), channel_id=1, source_target_pairs={{0,4},{4,8},{8,12},{12,16},{16,20},{20,24},{24,28},{28,0},{1,5},{5... | collective-permute-start | bytes 3538952 | tf_op jit(solution)/shard_map/ppermute | solution.py:12
Sparse Core Ops, SparseCore 0:
  8.9 40.1 all-gather.2
  50.6 539.4 all-gather.4
where the time goes:
time: 728 us
  waiting for transfers between devices  663 us (91%)
  matrix products  29.9 us (4%)
  local copies, waits for them, and re-layouts  13.4 us (2%)
  between operations  13.4 us (2%)
  other arithmetic  7.47 us (1%)
    all_gather x1, waiting for transfers between devices, on_device(): piece = lax.all_gather(qkv_weight, 'ctx', axis=0, tiled=True)  541 us
    ppermute x3, waiting for transfers between devices, shifted(): lax.ppermute(array, axis, [(i, (i + by) % devices) for i in range(devices)])  85.4 us
    all_gather x1, waiting for transfers between devices, on_device(): features = lax.all_gather(tokens, 'mp', axis=1, tiled=True)  35.7 us
    dot_general x1, matrix products, on_device(): jnp.dot(features, flat_piece, preferred_element_type=jnp.float32)  16.6 us
  transfers between devices with their start and end apart: 5, of which 5 were waited for; matrix products, arithmetic and copies ran while one was open for 1% of the time, Pallas kernels for 0%

commit v1 on v0

--- a/solution.py
+++ b/solution.py
@@ -27,7 +27,16 @@
     heads_local = qkv_weight.shape[2]
     head_size = qkv_weight.shape[3]
     scale = 1.0 / math.sqrt(head_size)
-    piece = lax.all_gather(qkv_weight, "ctx", axis=0, tiled=True)
+    array_2 = qkv_weight
+    ways, here, hop = (lax.axis_size("ctx"), lax.axis_index("ctx"), array_2.shape[0])
+    shape = [n * ways if d == 0 else n for d, n in enumerate(array_2.shape)]
+    full = lax.dynamic_update_slice_in_dim(
+        jnp.zeros(shape, array_2.dtype), array_2, here * hop, axis=0
+    )
+    for far in range(1, ways):
+        array_2 = lax.ppermute(array_2, "ctx", [(d, (d + 1) % ways) for d in range(ways)])
+        full = lax.dynamic_update_slice_in_dim(full, array_2, (here - far) % ways * hop, axis=0)
+    piece = full
     flat_piece = piece.reshape(piece.shape[0], -1)
     full_total = jnp.dot(features, flat_piece, preferred_element_type=jnp.float32)
     projected = full_total.astype(jnp.bfloat16).reshape(rows_dev, 3, heads_local, head_size)

time: 728 us -> 701 us (0.963)
  waiting for transfers between devices: 663 us -> 586 us
  local copies, waits for them, and re-layouts: 13.4 us -> 56.2 us
    all_gather x1 -> x0, waiting for transfers between devices: 541 us -> none  [on_device(): piece = lax.all_gather(qkv_weight, 'ctx', axis=0, tiled=True)]
    ppermute x0 -> x7, waiting for transfers between devices: none -> 515 us  [on_device(): lax.ppermute(array_2, 'ctx', [(d, (d + 1) % ways) for d in range(ways)])]
    all_gather x1, waiting for transfers between devices: 35.7 us -> 0.01 us  [on_device(): features = lax.all_gather(tokens, 'mp', axis=1, tiled=True)]
    dynamic_update_slice x0 -> x8, local copies, waits for them, and re-layouts: none -> 23.4 us  [the longest x7 21.2 us: on_device(): lax.dynamic_update_slice_in_dim(full, array_2, (here - far) % ways * hop,...]
    ppermute x3, waiting for transfers between devices: 85.4 us -> 71 us  [shifted(): lax.ppermute(array, axis, [(i, (i + by) % devices) for i in range(devices)])]
    unnamed x6 -> x24, local copies, waits for them, and re-layouts: 8.14 us -> 18.9 us
    broadcast_in_dim x0 -> x1, local copies, waits for them, and re-layouts: none -> 9.63 us  [on_device(): jnp.zeros(shape, array_2.dtype)]
  transfers between devices with their start and end apart: 5 -> 11, of which waited for: 5 -> 10; matrix products, arithmetic and copies ran while one was open for 1% -> 5% of each run, Pallas kernels for 0% -> 0%
where the time goes in v1:
time: 701 us; the launch traced here: 700 us
  waiting for transfers between devices  586 us (84%)
  local copies, waits for them, and re-layouts  56.2 us (8%)
  matrix products  33.5 us (5%)
  between operations  13.5 us (2%)
  other arithmetic  7.53 us (1%)
    ppermute x7, waiting for transfers between devices, on_device(): lax.ppermute(array_2, 'ctx', [(d, (d + 1) % ways) for d in range(ways)])  515 us
    ppermute x3, waiting for transfers between devices, shifted(): lax.ppermute(array, axis, [(i, (i + by) % devices) for i in range(devices)])  71 us
    dynamic_update_slice x7, local copies, waits for them, and re-layouts, on_device(): lax.dynamic_update_slice_in_dim(full, array_2, (here - far) % ways * hop,...  21.2 us
    dot_general x1, matrix products, on_device(): jnp.dot(features, flat_piece, preferred_element_type=jnp.float32)  20.2 us
    unnamed x24, local copies, waits for them, and re-layouts  18.9 us
  transfers between devices with their start and end apart: 11, of which 10 were waited for; matrix products, arithmetic and copies ran while one was open for 5% of the time, Pallas kernels for 0%

profile of v1, /device:TPU:0, one launch (start us, length us, event | category | flops | bytes accessed | tf_op | source)
XLA Modules:
  0.0 700.2 jit_solution(8765957279380406322)
XLA Ops:
  6.5 0.0 all-gather.2.cloned.1.call-start
  6.5 4.3 copy.7
  10.8 3.0 collective-permute-start
  13.8 79.6 %collective-permute-done = bf16[768,3,6,128]{0,3,2,1:T(8,128)(2,1)S(1)} collective-permute-done((bf16[768,3,6,128]{0,3,2,1:T(8,128)(2,1)S(1)}, bf16[768,3,6,128]{0,3,2,1:T(8,128)(2,1)S(1)}, u32[]{:S(2)}, u32[]{:S(2)}) %collective-permute-start) | collective-permute-done | bytes 3538976 | tf_op jit(solution)/shard_map/ppermute | solution.py:37
  93.4 0.0 copy-start
  93.4 1.7 copy-done
  95.1 0.0 collective-permute-start.1
  95.1 80.4 %collective-permute-done.1 = bf16[768,3,6,128]{0,3,2,1:T(8,128)(2,1)S(1)} collective-permute-done((bf16[768,3,6,128]{0,3,2,1:T(8,128)(2,1)S(1)}, bf16[768,3,6,128]{0,3,2,1:T(8,128)(2,1)S(1)}, u32[]{:S(2)}, u32[]{:S(2)}) %collective-permute-start.1) | collective-permute-done | bytes 3538976 | tf_op jit(solution)/shard_map/ppermute | solution.py:37
  175.5 0.0 copy-start.2
  175.5 1.8 copy-done.2
  177.4 0.0 collective-permute-start.2
  177.4 79.5 %collective-permute-done.2 = bf16[768,3,6,128]{0,3,2,1:T(8,128)(2,1)S(1)} collective-permute-done((bf16[768,3,6,128]{0,3,2,1:T(8,128)(2,1)S(1)}, bf16[768,3,6,128]{0,3,2,1:T(8,128)(2,1)S(1)}, u32[]{:S(2)}, u32[]{:S(2)}) %collective-permute-start.2) | collective-permute-done | bytes 3538976 | tf_op jit(solution)/shard_map/ppermute | solution.py:37
  256.9 0.0 copy-start.4
  256.9 1.8 copy-done.4
  258.7 0.0 collective-permute-start.3
  258.7 78.6 %collective-permute-done.3 = bf16[768,3,6,128]{0,3,2,1:T(8,128)(2,1)S(1)} collective-permute-done((bf16[768,3,6,128]{0,3,2,1:T(8,128)(2,1)S(1)}, bf16[768,3,6,128]{0,3,2,1:T(8,128)(2,1)S(1)}, u32[]{:S(2)}, u32[]{:S(2)}) %collective-permute-start.3) | collective-permute-done | bytes 3538976 | tf_op jit(solution)/shard_map/ppermute | solution.py:37
  337.2 0.0 copy-start.6
  337.2 1.9 copy-done.6
  339.1 0.0 collective-permute-start.4
  339.1 77.7 %collective-permute-done.4 = bf16[768,3,6,128]{0,3,2,1:T(8,128)(2,1)} collective-permute-done((bf16[768,3,6,128]{0,3,2,1:T(8,128)(2,1)S(1)}, bf16[768,3,6,128]{0,3,2,1:T(8,128)(2,1)}, u32[]{:S(2)}, u32[]{:S(2)}) %collective-permute-start.4) | collective-permute-done | bytes 3538976 | tf_op jit(solution)/shard_map/ppermute | solution.py:37
  416.9 0.0 collective-permute-start.5
  416.9 0.0 all-gather.2.cloned.1.call-update
  416.9 77.0 %collective-permute-done.5 = bf16[768,3,6,128]{0,3,2,1:T(8,128)(2,1)} collective-permute-done((bf16[768,3,6,128]{0,3,2,1:T(8,128)(2,1)}, bf16[768,3,6,128]{0,3,2,1:T(8,128)(2,1)}, u32[]{:S(2)}, u32[]{:S(2)}) %collective-permute-start.5) | collective-permute-done | bytes 3538976 | tf_op jit(solution)/shard_map/ppermute | solution.py:37
  493.9 0.0 collective-permute-start.6
  493.9 9.6 %broadcast_in_dim.2 = bf16[6144,3,6,128]{0,3,2,1:T(8,128)(2,1)} broadcast(bf16[]{:T(256)} %constant.59.clone.1), dimensions={} | broadcast | bytes 28311554 | tf_op jit(solution)/shard_map/broadcast_in_dim | solution.py:34
  503.5 0.0 copy-start.1
  503.5 2.2 constant_dynamic-update-slice_fusion.7
  505.8 1.0 copy-done.1
  506.8 0.0 copy-start.3
  506.8 2.0 constant_dynamic-update-slice_fusion.6
  508.9 1.2 copy-done.3
  510.1 0.0 copy-start.5
  510.1 2.2 constant_dynamic-update-slice_fusion.5
  512.3 1.0 copy-done.5
  513.4 2.0 constant_dynamic-update-slice_fusion.4
  515.4 1.2 copy-done.7
  516.6 2.3 constant_dynamic-update-slice_fusion.3
  519.0 4.3 constant_dynamic-update-slice_fusion.2
  523.2 4.1 constant_dynamic-update-slice_fusion.1
  527.4 42.7 %collective-permute-done.6 = bf16[768,3,6,128]{0,3,2,1:T(8,128)(2,1)} collective-permute-done((bf16[768,3,6,128]{0,3,2,1:T(8,128)(2,1)}, bf16[768,3,6,128]{0,3,2,1:T(8,128)(2,1)}, u32[]{:S(2)}, u32[]{:S(2)}) %collective-permute-start.6) | collective-permute-done | bytes 3538976 | tf_op jit(solution)/shard_map/ppermute | solution.py:37
  570.0 4.2 constant_dynamic-update-slice_fusion
  574.2 0.0 all-gather.2.cloned.1.call-done
  574.2 20.2 %convolution_convert_fusion = bf16[2304,384]{1,0:T(8,128)(2,1)S(1)} fusion(bf16[6144,2304]{0,1:T(8,128)(2,1)} %bitcast.31, bf16[384,6144]{1,0:T(8,128)(2,1)} %all-gather.2.cloned.1.call-done), kind=kOutput, calls=%fused_computation.7 | convolution fusion | flops 10872520704 | bytes 34799616 | tf_op jit(solution)/shard_map/dot_general | solution.py:41
  594.4 0.1 slice.44
  594.5 1.5 copy.15
  596.0 0.0 collective-permute-start.7
  596.0 26.3 %collective-permute-done.7 = bf16[384,2,6,128]{3,0,2,1:T(8,128)(2,1)S(1)} collective-permute-done((bf16[384,2,6,128]{3,0,2,1:T(8,128)(2,1)}, bf16[384,2,6,128]{3,0,2,1:T(8,128)(2,1)S(1)}, u32[]{:S(2)}, u32[]{:S(2)}) %collective-permute-start.7) | collective-permute-done | bytes 1179680 | tf_op jit(solution)/shard_map/ppermute | solution.py:12
  622.3 0.0 copy-start.8
  622.3 0.0 collective-permute-start.8
  622.3 25.9 %collective-permute-done.8 = bf16[384,2,6,128]{3,0,2,1:T(8,128)(2,1)} collective-permute-done((bf16[384,2,6,128]{3,0,2,1:T(8,128)(2,1)S(1)}, bf16[384,2,6,128]{3,0,2,1:T(8,128)(2,1)}, u32[]{:S(2)}, u32[]{:S(2)}) %collective-permute-start.8) | collective-permute-done | bytes 1179680 | tf_op jit(solution)/shard_map/ppermute | solution.py:12
  648.2 0.0 copy-done.8
  648.2 0.0 collective-permute-start.9
  648.3 0.1 fusion.33
  648.4 1.1 copy.16
  649.4 0.3 copy.14
  649.8 1.3 slice_bitcast_fusion.5
  651.1 1.3 slice_bitcast_fusion.4
  652.4 18.8 %collective-permute-done.9 = bf16[384,2,6,128]{3,0,2,1:T(8,128)(2,1)} collective-permute-done((bf16[384,2,6,128]{3,0,2,1:T(8,128)(2,1)}, bf16[384,2,6,128]{3,0,2,1:T(8,128)(2,1)}, u32[]{:S(2)}, u32[]{:S(2)}) %collective-permute-start.9) | collective-permute-done | bytes 1179680 | tf_op jit(solution)/shard_map/ppermute | solution.py:12
  671.2 1.3 slice_bitcast_fusion.3
  672.5 6.2 multiply_reduce_fusion
  678.7 0.0 copy-start.9
  678.7 7.5 %fusion = f32[6,384]{1,0:T(8,128)S(1)} fusion(f32[6,384,1536]{2,1,0:T(8,128)} %get-tuple-element.14, f32[6,384]{1,0:T(8,128)S(1)} %get-tuple-element.13), kind=kLoop, calls=%fused_computation.2 | loop fusion | flops 10614528 | bytes 14174208 | tf_op jit(solution)/shard_map/reduce_sum | solution.py:53
  686.2 0.0 copy-done.9
  686.2 7.1 %divide_convert_fusion = bf16[384,6,128]{2,0,1:T(8,128)(2,1)} fusion(bf16[384,6,128]{2,0,1:T(8,128)(2,1)S(1)} %get-tuple-element.12, bf16[384,6,128]{2,0,1:T(8,128)(2,1)S(1)} %get-tuple-element.10, bf16[384,6,128]{2,0,1:T(8,128)(2,1)S(1)} %get-tuple-element.8, bf16[384,6,128]{2,0,1:T(8,128)(2,1)S(1)} %bitcast.36, f32[6,384,1536]{2,1,0:T(8,128)} %get-tuple-element.14, ...), kind=kOutput, calls=%fused_computation.24 | convolution fusion | flops 926613504 | bytes 17123328 | tf_op jit(solution)/shard_map/hts,shd->htd/dot_general | solution.py:56
  (1 shorter events, 0.0 us)
Async XLA Ops:
  6.5 567.6 %all-gather.2.cloned.1.call-start = ((), (), s32[]{:S(2)}) async-start(), calls=%async_computation | async-start | bytes 5898240 | tf_op jit(solution)/shard_map/all_gather | solution.py:25
  10.8 82.6 %collective-permute-start = (bf16[768,3,6,128]{0,3,2,1:T(8,128)(2,1)S(1)}, bf16[768,3,6,128]{0,3,2,1:T(8,128)(2,1)S(1)}, u32[]{:S(2)}, u32[]{:S(2)}) collective-permute-start(bf16[768,3,6,128]{0,3,2,1:T(8,128)(2,1)S(1)} %copy.7), channel_id=1, source_target_pairs={{0,4},{4,8},{8,12},{12,16},{16,20},{20,24},{24,28},{28,0},{1,5},{5... | collective-permute-start | bytes 10616840 | tf_op jit(solution)/shard_map/ppermute | solution.py:37
  93.4 1.7 copy-start
  95.1 80.4 %collective-permute-start.1 = (bf16[768,3,6,128]{0,3,2,1:T(8,128)(2,1)S(1)}, bf16[768,3,6,128]{0,3,2,1:T(8,128)(2,1)S(1)}, u32[]{:S(2)}, u32[]{:S(2)}) collective-permute-start(bf16[768,3,6,128]{0,3,2,1:T(8,128)(2,1)S(1)} %collective-permute-done), channel_id=1, source_target_pairs={{0,4},{4,8},{8,12},{12,16},{16,20},{20,24},{24,28},{28,0},{1,5},{5... | collective-permute-start | bytes 10616840 | tf_op jit(solution)/shard_map/ppermute | solution.py:37
  175.5 1.8 copy-start.2
  177.4 79.5 %collective-permute-start.2 = (bf16[768,3,6,128]{0,3,2,1:T(8,128)(2,1)S(1)}, bf16[768,3,6,128]{0,3,2,1:T(8,128)(2,1)S(1)}, u32[]{:S(2)}, u32[]{:S(2)}) collective-permute-start(bf16[768,3,6,128]{0,3,2,1:T(8,128)(2,1)S(1)} %collective-permute-done.1), channel_id=1, source_target_pairs={{0,4},{4,8},{8,12},{12,16},{16,20},{20,24},{24,28},{28,0},{1,5},{5... | collective-permute-start | bytes 10616840 | tf_op jit(solution)/shard_map/ppermute | solution.py:37
  256.9 1.8 copy-start.4
  258.7 78.6 %collective-permute-start.3 = (bf16[768,3,6,128]{0,3,2,1:T(8,128)(2,1)S(1)}, bf16[768,3,6,128]{0,3,2,1:T(8,128)(2,1)S(1)}, u32[]{:S(2)}, u32[]{:S(2)}) collective-permute-start(bf16[768,3,6,128]{0,3,2,1:T(8,128)(2,1)S(1)} %collective-permute-done.2), channel_id=1, source_target_pairs={{0,4},{4,8},{8,12},{12,16},{16,20},{20,24},{24,28},{28,0},{1,5},{5... | collective-permute-start | bytes 10616840 | tf_op jit(solution)/shard_map/ppermute | solution.py:37
  337.2 1.9 copy-start.6
  339.1 77.8 %collective-permute-start.4 = (bf16[768,3,6,128]{0,3,2,1:T(8,128)(2,1)S(1)}, bf16[768,3,6,128]{0,3,2,1:T(8,128)(2,1)}, u32[]{:S(2)}, u32[]{:S(2)}) collective-permute-start(bf16[768,3,6,128]{0,3,2,1:T(8,128)(2,1)S(1)} %collective-permute-done.3), channel_id=1, source_target_pairs={{0,4},{4,8},{8,12},{12,16},{16,20},{20,24},{24,28},{28,0},{1,5},{5... | collective-permute-start | bytes 10616840 | tf_op jit(solution)/shard_map/ppermute | solution.py:37
  416.9 77.0 %collective-permute-start.5 = (bf16[768,3,6,128]{0,3,2,1:T(8,128)(2,1)}, bf16[768,3,6,128]{0,3,2,1:T(8,128)(2,1)}, u32[]{:S(2)}, u32[]{:S(2)}) collective-permute-start(bf16[768,3,6,128]{0,3,2,1:T(8,128)(2,1)} %collective-permute-done.4), channel_id=1, source_target_pairs={{0,4},{4,8},{8,12},{12,16},{16,20},{20,24},{24,28},{28,0},{1,5},{5... | collective-permute-start | bytes 10616840 | tf_op jit(solution)/shard_map/ppermute | solution.py:37
  493.9 76.1 %collective-permute-start.6 = (bf16[768,3,6,128]{0,3,2,1:T(8,128)(2,1)}, bf16[768,3,6,128]{0,3,2,1:T(8,128)(2,1)}, u32[]{:S(2)}, u32[]{:S(2)}) collective-permute-start(bf16[768,3,6,128]{0,3,2,1:T(8,128)(2,1)} %collective-permute-done.5), channel_id=1, source_target_pairs={{0,4},{4,8},{8,12},{12,16},{16,20},{20,24},{24,28},{28,0},{1,5},{5... | collective-permute-start | bytes 10616840 | tf_op jit(solution)/shard_map/ppermute | solution.py:37
  503.5 3.3 copy-start.1
  506.8 3.3 copy-start.3
  510.1 3.3 copy-start.5
  513.4 3.3 copy-start.7
  596.0 26.3 %collective-permute-start.7 = (bf16[384,2,6,128]{3,0,2,1:T(8,128)(2,1)}, bf16[384,2,6,128]{3,0,2,1:T(8,128)(2,1)S(1)}, u32[]{:S(2)}, u32[]{:S(2)}) collective-permute-start(bf16[384,2,6,128]{3,0,2,1:T(8,128)(2,1)} %copy.15), channel_id=1, source_target_pairs={{0,4},{4,8},{8,12},{12,16},{16,20},{20,24},{24,28},{28,0},{1,5},{5... | collective-permute-start | bytes 3538952 | tf_op jit(solution)/shard_map/ppermute | solution.py:12
  622.3 25.9 %copy-start.8 = (bf16[384,2,6,128]{3,0,2,1:T(8,128)(2,1)}, bf16[384,2,6,128]{3,0,2,1:T(8,128)(2,1)S(1)}, u32[]{:S(2)}) copy-start(bf16[384,2,6,128]{3,0,2,1:T(8,128)(2,1)S(1)} %collective-permute-done.7) | copy-start | bytes 3538948
  622.3 25.9 %collective-permute-start.8 = (bf16[384,2,6,128]{3,0,2,1:T(8,128)(2,1)S(1)}, bf16[384,2,6,128]{3,0,2,1:T(8,128)(2,1)}, u32[]{:S(2)}, u32[]{:S(2)}) collective-permute-start(bf16[384,2,6,128]{3,0,2,1:T(8,128)(2,1)S(1)} %collective-permute-done.7), channel_id=1, source_target_pairs={{0,4},{4,8},{8,12},{12,16},{16,20},{20,24},{24,28},{28,0},{1,5},{5... | collective-permute-start | bytes 3538952 | tf_op jit(solution)/shard_map/ppermute | solution.py:12
  648.2 22.9 %collective-permute-start.9 = (bf16[384,2,6,128]{3,0,2,1:T(8,128)(2,1)}, bf16[384,2,6,128]{3,0,2,1:T(8,128)(2,1)}, u32[]{:S(2)}, u32[]{:S(2)}) collective-permute-start(bf16[384,2,6,128]{3,0,2,1:T(8,128)(2,1)} %collective-permute-done.8), channel_id=1, source_target_pairs={{0,4},{4,8},{8,12},{12,16},{16,20},{20,24},{24,28},{28,0},{1,5},{5... | collective-permute-start | bytes 3538952 | tf_op jit(solution)/shard_map/ppermute | solution.py:12
  678.7 7.5 %copy-start.9 = (bf16[384,1,6,128]{3,0,2,1:T(8,128)(2,1)S(1)}, bf16[384,1,6,128]{3,0,2,1:T(8,128)(2,1)}, u32[]{:S(2)}) copy-start(bf16[384,1,6,128]{3,0,2,1:T(8,128)(2,1)} %copy.16) | copy-start | bytes 1769476
Sparse Core Ops, SparseCore 0:
  417.0 38.1 all-gather.1
